TPU v7x, 512 devices: a whole 4x8x8 slice. The times are simulated.
512 devices in a mesh: row: 16 (over y, x_lo), col: 32 (over z, x_hi, core).
Axes of the slice: x: 4 (x_hi: 2, x_lo: 2; x = x_hi * 2 + x_lo), y: 8, z: 8, core: 2. Of those that a mesh axis runs over, the one named last changes fastest.
Arguments:
- features: bfloat16 [65536, 128], P(('col', 'row')), may hold values from -6 to 6
- block_ids: int32 [16, 32, 32], P('row', 'col'), may hold values from 0 to 511
- block_values: bfloat16 [16, 32, 32, 128, 128], P('row', 'col'), as said below
- block_count: int32 [16, 32], P('row', 'col'), may hold values from 8 to 32, as said below
- labels: int32 [65536], P(('col', 'row')), may hold values from 0 to 171
- w_first: bfloat16 [128, 512], replicated, may hold values from -0.5 to 0.5
- w_second: bfloat16 [512, 172], replicated, may hold values from -0.25 to 0.25
Outputs:
- logits: float32 [65536, 172], P(('col', 'row'))
- grad_first: float32 [128, 512], replicated
- grad_second: float32 [512, 172], replicated
Inputs may be any that keep to these rules, and one draw needn't show every extreme that they name: Only the first block_count slots of a tile are blocks of the graph; every tile has at least a quarter of its 32 slots live, and some tile has all of them. `block_ids`: A position may be listed more than once in a tile. `block_values`: entries are nonnegative.
All inputs are finite; a program needn't handle non-finite values.
Results may differ from a plain program's by a relative error of at most 0.0033.
Values may be sent and summed in bfloat16 or wider, within the bound.
A program may use at most 64 MiB of HBM per device.

v0:
```python
import jax
import jax.numpy as jnp
from jax import lax
from jax.sharding import PartitionSpec as P

BLOCK = 128


def forward_term(values, block_ids, panel, row_blocks, col_blocks):
    width = panel.shape[-1]
    picked = panel.reshape(col_blocks, BLOCK, width)[block_ids % col_blocks]
    products = jnp.einsum("bij,bjf->bif", values, picked, preferred_element_type=jnp.float32)
    summed = jax.ops.segment_sum(products, block_ids // col_blocks, num_segments=row_blocks)
    return summed.reshape(row_blocks * BLOCK, width)


def reverse_term(values, block_ids, panel, row_blocks, col_blocks):
    width = panel.shape[-1]
    picked = panel.reshape(row_blocks, BLOCK, width)[block_ids // col_blocks]
    products = jnp.einsum("bji,bjf->bif", values, picked, preferred_element_type=jnp.float32)
    summed = jax.ops.segment_sum(products, block_ids % col_blocks, num_segments=col_blocks)
    return summed.reshape(col_blocks * BLOCK, width)


def shards(features, block_ids, block_values, block_count, labels, w_first, w_second):
    slot_ids = block_ids[0, 0]
    live_count = block_count[0, 0]
    alive = jnp.arange(slot_ids.shape[0]) < live_count
    values = jnp.where(alive[:, None, None], block_values[0, 0], jnp.zeros((), jnp.bfloat16))
    nodes_dev = features.shape[0]
    row_blocks = nodes_dev * lax.axis_size("col") // BLOCK
    col_blocks = nodes_dev * lax.axis_size("row") // BLOCK
    col_features = lax.all_gather(features, "row", axis=0, tiled=True)
    first_term = forward_term(values, slot_ids, col_features, row_blocks, col_blocks)
    agg_first = lax.psum_scatter(first_term, "col", scatter_dimension=0, tiled=True).astype(
        jnp.bfloat16
    )
    pre_first = jnp.dot(agg_first, w_first, preferred_element_type=jnp.float32)
    hidden = jnp.maximum(pre_first, 0.0).astype(jnp.bfloat16)
    second_in = jnp.dot(hidden, w_second, preferred_element_type=jnp.float32).astype(jnp.bfloat16)
    row_second = lax.all_gather(second_in, "col", axis=0, tiled=True)
    second_term = reverse_term(values, slot_ids, row_second, row_blocks, col_blocks)
    logits = lax.psum_scatter(second_term, "row", scatter_dimension=0, tiled=True)
    top = jnp.max(logits, axis=1, keepdims=True)
    expo = jnp.exp(logits - top)
    prob = expo / jnp.sum(expo, axis=1, keepdims=True)
    onehot = (labels[:, None] == jnp.arange(logits.shape[1], dtype=jnp.int32)[None, :]).astype(
        jnp.float32
    )
    d_logits = (prob - onehot).astype(jnp.bfloat16)
    col_grads = lax.all_gather(d_logits, "row", axis=0, tiled=True)
    grad_term = forward_term(values, slot_ids, col_grads, row_blocks, col_blocks)
    d_second = lax.psum_scatter(
        grad_term.astype(jnp.bfloat16), "col", scatter_dimension=0, tiled=True
    )
    d_hidden = jnp.dot(d_second, w_second.T, preferred_element_type=jnp.float32)
    d_pre = jnp.where(pre_first > 0.0, d_hidden, jnp.zeros_like(d_hidden)).astype(jnp.bfloat16)
    part_first = jnp.einsum("nf,nh->fh", agg_first, d_pre, preferred_element_type=jnp.float32)
    part_second = jnp.einsum("nh,nk->hk", hidden, d_second, preferred_element_type=jnp.float32)
    grad_first, grad_second = lax.psum((part_first, part_second), ("row", "col"))
    return (logits, grad_first, grad_second)


def solution(mesh):
    in_specs = (
        P(("col", "row"), None),
        P("row", "col", None),
        P("row", "col", None, None, None),
        P("row", "col"),
        P(("col", "row")),
        P(),
        P(),
    )
    out_specs = (P(("col", "row"), None), P(), P())
    return jax.shard_map(shards, mesh=mesh, in_specs=in_specs, out_specs=out_specs, check_vma=False)
```

profile of v0, /device:TPU:1, one launch (start us, length us, event | category | flops | bytes accessed | tf_op | source)
XLA Modules:
  0.0 825.7 jit_solution(5422737758304434975)
XLA Ops:
  7.2 0.0 copy-start
  7.2 0.0 copy-start.2
  7.2 0.0 reduce-scatter.6.cloned.1.call-start
  8.0 0.7 fusion.10
  8.7 31.0 %all_gather.9 = bf16[2048,128]{1,0:T(8,128)(2,1)S(1)} all-gather(bf16[128,128]{1,0:T(8,128)(2,1)} %param.7), channel_id=1, replica_groups=mesh['row'=16,'col'=32] {'row'}, dimensions={0}, use_global_device_ids=true | all-gather | bytes 557056 | tf_op jit(solution)/shard_map/all_gather | solution.py:33
  39.7 0.7 gather_fusion
  40.5 0.0 copy-done.2
  40.5 1.8 fusion.17
  42.3 0.2 broadcast_in_dim.21
  42.5 4.7 scatter_fusion
  47.2 0.0 copy-start.1
  47.2 0.0 copy-start.6
  47.2 1.3 copy-done.1
  48.6 0.0 reduce-scatter.6.cloned.1.call-update
  48.6 0.0 all-gather.2.cloned.1.call-start
  48.6 132.1 %reduce-scatter.6.cloned.1.call-done = f32[128,128]{1,0:T(8,128)} async-done(((f32[4096,128]{1,0:T(8,128)}), f32[128,128]{1,0:T(8,128)}) %reduce-scatter.6.cloned.1.call-update) | async-done | bytes 65552 | tf_op jit(solution)/shard_map/reduce_scatter | solution.py:35
  180.7 0.0 copy-done.6
  180.7 1.0 fusion.7
  181.8 0.0 copy-start.3
  181.8 0.7 copy-done.3
  182.5 0.0 copy-done
  182.5 0.8 convolution_convert_fusion
  183.3 0.0 all-gather.2.cloned.1.call-update
  183.3 0.0 reduce-scatter.8.cloned.1.call-start
  183.4 84.2 %all-gather.2.cloned.1.call-done = bf16[4096,172]{0,1:T(8,128)(2,1)} async-done(((bf16[128,172]{0,1:T(8,128)(2,1)}), bf16[4096,172]{0,1:T(8,128)(2,1)}) %all-gather.2.cloned.1.call-update) | async-done | bytes 1409040 | tf_op jit(solution)/shard_map/all_gather | solution.py:41
  267.6 1.7 copy.28
  269.2 0.2 slice_bitcast_fusion
  269.5 0.5 copy.21
  270.0 1.8 gather_fusion.1
  271.9 3.5 fusion.16
  275.4 0.1 broadcast_in_dim.18
  275.5 5.4 scatter_fusion.1
  280.9 0.5 copy.34
  281.3 0.1 pad.3
  281.5 0.0 copy-start.7
  281.5 1.7 copy.29
  283.1 0.0 reduce-scatter.8.cloned.1.call-update
  283.1 0.0 reduce-scatter.10.cloned.1.call-start
  283.2 61.0 %reduce-scatter.8.cloned.1.call-done = f32[128,172]{0,1:T(8,128)} async-done(((f32[2048,172]{0,1:T(8,128)}), f32[128,172]{0,1:T(8,128)}) %reduce-scatter.8.cloned.1.call-update) | async-done | bytes 88080 | tf_op jit(solution)/shard_map/reduce_scatter | solution.py:43
  344.2 0.9 reduce_max.9
  345.1 0.9 fusion.4
  346.1 0.0 copy-done.7
  346.1 0.9 subtract_convert_fusion
  347.0 28.1 %all_gather.11 = bf16[2048,172]{0,1:T(8,128)(2,1)S(1)} all-gather(bf16[128,172]{0,1:T(8,128)(2,1)S(1)} %subtract_convert_fusion), channel_id=1, replica_groups=mesh['row'=16,'col'=32] {'row'}, dimensions={0}, use_global_device_ids=true | all-gather | bytes 748544 | tf_op jit(solution)/shard_map/all_gather | solution.py:51
  375.1 0.1 copy.30
  375.3 0.1 slice_bitcast_fusion.1
  375.4 0.2 copy.23
  375.6 0.8 gather_fusion.2
  376.4 2.6 fusion.15
  379.0 0.2 broadcast_in_dim.36
  379.2 5.4 scatter_fusion.2
  384.5 2.0 copy.33
  386.5 4.1 copy.27
  390.7 0.0 reduce-scatter.10.cloned.1.call-update
  390.7 0.0 all-reduce.3.cloned.1.call-start
  390.8 141.9 %reduce-scatter.10.cloned.1.call-done = bf16[128,172]{1,0:T(8,128)(2,1)} async-done(((bf16[4096,172]{1,0:T(8,128)(2,1)}), bf16[128,172]{1,0:T(8,128)(2,1)}) %reduce-scatter.10.cloned.1.call-update) | async-done | bytes 44048
  532.7 0.0 copy-done.4
  532.7 0.0 copy-done.5
  532.7 1.9 fusion.1
  534.5 1.8 fusion.5
  536.4 0.0 all-reduce.3.cloned.1.call-update
  536.4 279.4 %all-reduce.3.cloned.1.call-done = (f32[128,512]{1,0:T(8,128)}, f32[512,172]{0,1:T(8,128)}) async-done(((f32[128,512]{1,0:T(8,128)}, f32[512,172]{0,1:T(8,128)}), (f32[128,512]{1,0:T(8,128)}, f32[512,172]{0,1:T(8,128)})) %all-reduce.3.cloned.1.call-update) | async-done | bytes 614416 | tf_op jit(solution)/shard_map/psum | solution.py:60
  815.8 1.7 copy.41
  817.5 1.7 copy.42
  (6 shorter events, 0.0 us)
Async XLA Ops:
  7.2 175.3 %copy-start = (bf16[512,172]{0,1:T(8,128)(2,1)S(1)}, bf16[512,172]{0,1:T(8,128)(2,1)}, u32[]{:S(2)}) copy-start(bf16[512,172]{0,1:T(8,128)(2,1)} %param.13) | copy-start | bytes 528388
  7.2 33.3 %copy-start.2 = (bf16[1,1,32,128,128]{4,3,2,1,0:T(8,128)(2,1)S(1)}, bf16[1,1,32,128,128]{4,3,2,1,0:T(8,128)(2,1)}, u32[]{:S(2)}) copy-start(bf16[1,1,32,128,128]{4,3,2,1,0:T(8,128)(2,1)} %param.9) | copy-start | bytes 3145732
  7.2 173.5 %reduce-scatter.6.cloned.1.call-start = ((), (), s32[]{:S(2)}) async-start(), calls=%async_computation.3 | async-start | bytes 2162688 | tf_op jit(solution)/shard_map/reduce_scatter | solution.py:35
  47.2 1.3 copy-start.1
  47.2 133.5 %copy-start.6 = (bf16[128,512]{1,0:T(8,128)(2,1)S(1)}, bf16[128,512]{1,0:T(8,128)(2,1)}, u32[]{:S(2)}) copy-start(bf16[128,512]{1,0:T(8,128)(2,1)} %param.12) | copy-start | bytes 393220
  48.6 219.0 %all-gather.2.cloned.1.call-start = ((), (), s32[]{:S(2)}) async-start(), calls=%async_computation.4 | async-start | bytes 1486848 | tf_op jit(solution)/shard_map/all_gather | solution.py:41
  181.8 0.7 copy-start.3
  183.3 160.9 %reduce-scatter.8.cloned.1.call-start = ((), (), s32[]{:S(2)}) async-start(), calls=%async_computation.5 | async-start | bytes 1531904 | tf_op jit(solution)/shard_map/reduce_scatter | solution.py:43
  281.5 64.6 %copy-start.7 = (s32[128]{0:T(128)S(1)}, s32[128]{0:T(128)}, u32[]{:S(2)}) copy-start(s32[128]{0:T(128)} %param.11) | copy-start | bytes 1540
  283.1 249.5 %reduce-scatter.10.cloned.1.call-start = ((), (), s32[]{:S(2)}) async-start(), calls=%async_computation.6 | async-start | bytes 2162688
  386.5 146.1 %copy-start.4 = (f32[128,512]{1,0:T(8,128)S(1)}, f32[128,512]{1,0:T(8,128)}, u32[]{:S(2)}) copy-start(f32[128,512]{1,0:T(8,128)} %copy-done.3) | copy-start | bytes 786436
  386.5 146.1 %copy-start.5 = (f32[128,128]{1,0:T(8,128)S(1)}, f32[128,128]{1,0:T(8,128)}, u32[]{:S(2)}) copy-start(f32[128,128]{1,0:T(8,128)} %reduce-scatter.6.cloned.1.call-done) | copy-start | bytes 196612
  390.7 425.1 %all-reduce.3.cloned.1.call-start = ((), (), s32[]{:S(2)}) async-start(), calls=%async_computation.7 | async-start | bytes 1245184 | tf_op jit(solution)/shard_map/psum | solution.py:60
Sparse Core Ops, SparseCore 0:
  48.7 131.9 reduce-scatter.5
  184.5 83.0 all-gather.1
  283.3 60.8 reduce-scatter.7
  390.8 141.7 reduce-scatter.9
  538.3 277.4 all-reduce.2
where the time goes:
time: 827 us; the launch traced here: 826 us
  waiting for transfers between devices  699 us (85%)
  blocking collectives  59.1 us (7%)
  local copies, waits for them, and re-layouts  20.6 us (2%)
  other arithmetic  18.9 us (2%)
  between operations  14.7 us (2%)
  matrix products  13.5 us (2%)
    psum x1, waiting for transfers between devices, shards(): lax.psum((part_first, part_second), ('row', 'col'))  279 us
    unnamed x6, waiting for transfers between devices  142 us
    reduce_scatter x1, waiting for transfers between devices, shards(): lax.psum_scatter(first_term, 'col', scatter_dimension=0, tiled=True)  132 us
    all_gather x1, waiting for transfers between devices, shards(): row_second = lax.all_gather(second_in, 'col', axis=0, tiled=True)  84.2 us
    reduce_scatter x1, waiting for transfers between devices, shards(): lax.psum_scatter(second_term, 'row', scatter_dimension=0, tiled=True)  61 us
    all_gather x1, blocking collectives, shards(): col_features = lax.all_gather(features, 'row', axis=0, tiled=True)  31 us
    all_gather x1, blocking collectives, shards(): col_grads = lax.all_gather(d_logits, 'row', axis=0, tiled=True)  28.1 us
  transfers between devices with their start and end apart: 5, of which 5 were waited for; matrix products, arithmetic and copies ran while one was open for 0% of the time, Pallas kernels for 0%

commit v1 on v0

v1 whole, which is shorter than its diff:
```python
import jax
import jax.numpy as jnp
from jax import lax
from jax.experimental import pallas as pl
from jax.experimental.pallas import tpu as pltpu
from jax.sharding import PartitionSpec as P

MESH = pl.DeviceIdType.MESH
BLOCK = 128
CLASSES = 172
WIDE = 176
OFFSETS = (4, 3, 5, 2, 6, 1, 7)
NEAR = tuple(reversed(range(7)))
F32 = jnp.float32
BF16 = jnp.bfloat16
VM = pl.BlockSpec(memory_space=pltpu.VMEM)
SM = pl.BlockSpec(memory_space=pltpu.SMEM)
ANY = pl.BlockSpec(memory_space=pl.ANY)
DMA = pltpu.SemaphoreType.DMA


class Place:
    def __init__(self):
        self.row = lax.axis_index("row")
        self.col = lax.axis_index("col")
        self.y = self.row // 2
        self.xl = self.row % 2
        self.z = self.col // 4
        self.xh = (self.col // 2) % 2
        self.core = self.col % 2

    def along_y(self, offset):
        return (self.y + offset) % 8

    def along_z(self, offset):
        return (self.z + offset) % 8

    def y_peer(self, offset):
        return (self.along_y(offset) * 2 + self.xl, self.col)

    def z_peer(self, offset):
        return (self.row, self.along_z(offset) * 4 + self.xh * 2 + self.core)

    def lo_peer(self):
        return (self.y * 2 + 1 - self.xl, self.col)

    def hi_peer(self):
        return (self.row, self.z * 4 + (1 - self.xh) * 2 + self.core)

    def twin(self):
        return (self.row, self.z * 4 + self.xh * 2 + 1 - self.core)

    def row_peer(self, offset):
        return ((self.row + offset) % 16, self.col)

    def half(self):
        return self.z * 2 + self.xh

    def half_peer(self, offset):
        return (self.row, ((self.half() + offset) % 16) * 2 + self.core)


def send(src, dst, send_sem, recv_sem, peer):
    copy = pltpu.make_async_remote_copy(
        src_ref=src, dst_ref=dst, send_sem=send_sem, recv_sem=recv_sem, device_id=peer, device_id_type=MESH
    )
    copy.start()
    return copy


def greet(peers):
    barrier = pltpu.get_barrier_semaphore()
    for peer in peers:
        pl.semaphore_signal(barrier, inc=1, device_id=peer, device_id_type=MESH)
    pl.semaphore_wait(barrier, len(peers))


def gather_row(me, own, panel, y_send, y_recv, x_send, x_recv, work=None):
    index = me.row
    first = send(own, panel.at[index], x_send.at[7], x_recv.at[7], me.lo_peer())
    along = [None] * 7
    for i in NEAR:
        along[i] = send(own, panel.at[index], y_send.at[i], y_recv.at[i], me.y_peer(OFFSETS[i]))
    local = pltpu.make_async_copy(own, panel.at[index], y_send.at[7])
    local.start()
    if work is not None:
        work()
    across = [first]
    for i in NEAR:
        along[i].wait_recv()
        source = me.along_y(8 - OFFSETS[i]) * 2 + me.xl
        across.append(send(panel.at[source], panel.at[source], x_send.at[i], x_recv.at[i], me.lo_peer()))
    local.wait()
    for copy in across:
        copy.wait_recv()
    return along + across


def encode(value, ref, index):
    near = (jnp.sum(value, axis=0, keepdims=True) * (1.0 / BLOCK)).astype(BF16)
    ref[index, :BLOCK, :] = (value - near.astype(F32)).astype(BF16)
    ref[index, BLOCK:, :] = jnp.broadcast_to(near, (16, BLOCK))


def decode(ref, index):
    return ref[index, :BLOCK, :].astype(F32) + ref[index, BLOCK:, :].astype(F32)[:1]


def sum_by_slot(table, links, acc, product):
    def multiply(s, carry):
        acc[s + 1] = product(s)
        return carry

    lax.fori_loop(0, 32, multiply, 0, unroll=8)

    def chain(s, carry):
        acc[s + 1] = acc[s + 1] + acc[table[links, s]]
        return carry

    lax.fori_loop(0, 32, chain, 0, unroll=4)


def reduce_all(me, a_in, b_in, a_out, b_out, a_twin, b_twin, a_half, b_half, a_cut, b_cut, a_got, b_got, a_all, b_all,
               send_sem, recv_sem):
    lanes = ((a_in, a_out, a_twin, a_half, a_cut, a_got, a_all, 24, me.row_peer, me.row, me.half_peer, me.half()),
             (b_in, b_out, b_twin, b_half, b_cut, b_got, b_all, 16, me.half_peer, me.half(), me.row_peer, me.row))

    def rows(index, size):
        return pl.ds(pl.multiple_of(index * size, 8), size)

    def settle(ref, stage, which):
        return pltpu.make_async_remote_copy(
            src_ref=ref, dst_ref=ref, send_sem=send_sem.at[stage, which], recv_sem=recv_sem.at[stage, which],
            device_id=me.twin(), device_id_type=MESH)

    swaps = []
    for which, (source, out, twin, half, cut, got, every, size, peer1, at1, peer2, at2) in enumerate(lanes):
        swaps.append(send(source.at[rows(1 - me.core, 16 * size)], twin, send_sem.at[0, which], recv_sem.at[0, which], me.twin()))
    for which, (source, out, twin, half, cut, got, every, size, peer1, at1, peer2, at2) in enumerate(lanes):
        swaps[which].wait_recv()
        half[...] = source[rows(me.core, 16 * size), :] + twin[...]
        for k in range(16):
            cut[k] = half[k * size:(k + 1) * size, :].astype(BF16)
        for k in range(1, 16):
            send(cut.at[(at1 + k) % 16], got.at[k - 1], send_sem.at[1, which], recv_sem.at[1, which], peer1(k))
    for which, (source, out, twin, half, cut, got, every, size, peer1, at1, peer2, at2) in enumerate(lanes):
        settle(got, 1, which).wait_recv()
        total = half[rows(at1, size), :]
        for k in range(15):
            total = total + got[k].astype(F32)
        every[at2] = total.astype(BF16)
        for k in range(1, 16):
            send(every.at[at2], every.at[at2], send_sem.at[2, which], recv_sem.at[2, which], peer2(k))
    for which, (source, out, twin, half, cut, got, every, size, peer1, at1, peer2, at2) in enumerate(lanes):
        settle(got, 2, which).wait_recv()
        total = every[0].astype(F32)
        for k in range(1, 16):
            total = total + every[k].astype(F32)
        place = rows(me.core * 16 + at1, size)
        out[place, :] = total
        for k in range(1, 16):
            send(out.at[place], out.at[place], send_sem.at[3, which], recv_sem.at[3, which], peer1(k))
    last = []
    for which, (source, out, twin, half, cut, got, every, size, peer1, at1, peer2, at2) in enumerate(lanes):
        settle(out.at[pl.ds(0, 15 * size)], 3, which).wait_recv()
        part = out.at[rows(me.core, 16 * size)]
        last.append(send(part, part, send_sem.at[4, which], recv_sem.at[4, which], me.twin()))
    for copy in last:
        copy.wait_recv()
    for which, (source, out, twin, half, cut, got, every, size, peer1, at1, peer2, at2) in enumerate(lanes):
        swaps[which].wait_send()
        settle(got, 1, which).wait_send()
        settle(got, 2, which).wait_send()
        settle(out.at[pl.ds(0, 15 * size)], 3, which).wait_send()
        last[which].wait_send()


def link_tables(ids, ids_wide, count, rows, table_v, table_s, sem):
    rows[...] = jnp.zeros_like(rows)
    rows[0:1, 0:32] = ids_wide[...]
    every = rows[0:1, :]
    lane = lax.broadcasted_iota(jnp.int32, (1, BLOCK), 1)
    none = jnp.zeros((1, BLOCK), jnp.int32)

    def row_place(x):
        r = x // 16
        return (r % 2) * 16 + ((r // 2) % 2) * 8 + r // 4

    def col_place(x):
        return (x % 2) * 8 + (x % 16) // 2

    row_every, col_every = row_place(every), col_place(every)

    def add(t, carry):
        row_before, row_last, col_before, col_last = carry
        row, col = row_place(ids[0, t]), col_place(ids[0, t])
        late = (lane > t) & (t < count)
        alive = (lane >= 0) & (t < count)
        return (jnp.where(late & (row_every == row), t + 1, row_before), jnp.where(alive & (lane == row), t + 1, row_last),
                jnp.where(late & (col_every == col), t + 1, col_before), jnp.where(alive & (lane == col), t + 1, col_last))

    row_before, row_last, col_before, col_last = lax.fori_loop(0, 32, add, (none, none, none, none))
    for at, line in enumerate((every % 16, row_before, row_last, row_every, col_before, col_last)):
        table_v[at:at + 1, :] = line
    copy = pltpu.make_async_copy(table_v, table_s, sem)
    copy.start()
    return copy


def everything(features, ids, ids_wide, count, values_any, labels, w1_any, w2_in, logits_t, b_out, a_out,
               rows, table_v, table, values, w1, w2, panel, acc, part, from_twin, to_hi, from_hi, to_z, from_z, agg,
               hidden, second, acc_wide, to_x, from_x, to_y, from_y, grads, panel_wide, grad,
               acc_first, acc_second, a_in, b_in, a_twin, b_twin, a_half, b_half, a_cut, b_cut, a_got, b_got, a_all, b_all,
               load, fs_y, fr_y, fs_x, fr_x, c_send, c_recv, h_send, h_recv, z_send, z_recv,
               ac_send, ac_recv, ah_send, ah_recv, az_send, az_recv, x_send, x_recv, y_send, y_recv,
               ax_send, ax_recv, ay_send, ay_recv, send_sem, recv_sem):
    me = Place()
    barrier = pltpu.get_barrier_semaphore()
    peers = [me.twin()] + [me.row_peer(k) for k in range(1, 16)] + [me.half_peer(k) for k in range(1, 16)]
    for peer in peers:
        pl.semaphore_signal(barrier, inc=1, device_id=peer, device_id_type=MESH)
    loads = [pltpu.make_async_copy(src, dst, load.at[i]) for i, (src, dst) in
             enumerate(((values_any.at[0, 0], values), (w1_any, w1)))]
    for copy in loads:
        copy.start()
    tabled = link_tables(ids, ids_wide, count[0, 0], rows, table_v, table, load.at[3])
    w2[...] = jnp.zeros_like(w2)
    w2[:CLASSES, :] = w2_in[...]
    acc[0] = jnp.zeros(acc.shape[1:], F32)
    acc_wide[0] = jnp.zeros(acc_wide.shape[1:], F32)
    pl.semaphore_wait(barrier, len(peers))
    sent = []
    sent += gather_row(me, features, panel, fs_y, fr_y, fs_x, fr_x)
    for copy in loads:
        copy.wait()
    tabled.wait()

    sum_by_slot(table, 1, acc, lambda s: jnp.dot(values[s], panel[table[0, s]], preferred_element_type=F32))
    mine, theirs = me.core * 16, (1 - me.core) * 16
    near, far = me.xh * 8, (1 - me.xh) * 8

    def partial(at):
        return acc[table[2, at]]

    halves = []
    for k, side in enumerate((far, near)):
        for q in range(8):
            part[k * 8 + q] = partial(theirs + side + q)
        halves.append(send(part.at[pl.ds(k * 8, 8)], from_twin.at[pl.ds(side, 8)], c_send.at[k], c_recv.at[k], me.twin()))
    halves[0].wait_recv()
    hops = []
    for i, step in enumerate(OFFSETS + (0,)):
        at = me.along_z(step)
        encode(partial(mine + far + at) + from_twin[far + at], to_hi, at)
        hops.append(send(to_hi.at[at], from_hi.at[at], h_send.at[i], h_recv.at[i], me.hi_peer()))
    halves[1].wait_recv()
    rounds = []
    for i, step in enumerate(OFFSETS):
        at = me.along_z(step)
        hops[i].wait_recv()
        encode(partial(mine + near + at) + from_twin[near + at] + decode(from_hi, at), to_z, at)
        rounds.append(send(to_z.at[at], from_z.at[i], z_send.at[i], z_recv.at[i], me.z_peer(step)))
    hops[7].wait_recv()
    total = partial(mine + near + me.z) + from_twin[near + me.z] + decode(from_hi, me.z)
    for i in range(7):
        rounds[i].wait_recv()
        total = total + decode(from_z, i)
    own = mine + near + me.z
    agg[own] = total.astype(BF16)
    sent += halves + hops + rounds

    def dense(places):
        pre = jnp.dot(jnp.concatenate([agg[at] for at in places], axis=0), w1[...], preferred_element_type=F32)
        kept = jnp.maximum(pre, 0.0).astype(BF16)
        turned = lax.dot_general(w2[...], kept, (((1,), (1,)), ((), ())), preferred_element_type=F32).astype(BF16)
        for k, at in enumerate(places):
            hidden[at] = kept[k * BLOCK:(k + 1) * BLOCK]
            second[at] = turned[:, k * BLOCK:(k + 1) * BLOCK]

    block = agg.at[own]
    across = [None] * 8
    along = [None] * 7
    twins = [None] * 16
    across[7] = send(block, block, ah_send.at[7], ah_recv.at[7], me.hi_peer())
    for i in NEAR:
        along[i] = send(block, block, az_send.at[i], az_recv.at[i], me.z_peer(OFFSETS[i]))
    twins[15] = send(block, block, ac_send.at[15], ac_recv.at[15], me.twin())
    across[7].wait_recv()
    other = mine + far + me.z
    twins[14] = send(agg.at[other], agg.at[other], ac_send.at[14], ac_recv.at[14], me.twin())
    ready = [own, other]
    late = [(15, theirs + near + me.z), (14, theirs + far + me.z)]
    for step in (((0, 6), (0, 5)), ((0, 4), (0, 3)), ((1, 6), (1, 5)), ((0, 2), (0, 1)), ((1, 4), (1, 3)), ((0, 0), (1, 2)),
                 ((1, 1), (1, 0)), ()):
        for over_x, i in step:
            source = me.along_z(8 - OFFSETS[i])
            if over_x:
                across[i].wait_recv()
                at = mine + far + source
                twins[7 + i] = send(agg.at[at], agg.at[at], ac_send.at[7 + i], ac_recv.at[7 + i], me.twin())
                late.append((7 + i, theirs + far + source))
            else:
                along[i].wait_recv()
                at = mine + near + source
                across[i] = send(agg.at[at], agg.at[at], ah_send.at[i], ah_recv.at[i], me.hi_peer())
                twins[i] = send(agg.at[at], agg.at[at], ac_send.at[i], ac_recv.at[i], me.twin())
                late.append((i, theirs + near + source))
            ready.append(at)
        while len(ready) < 4:
            k, at = late.pop(0)
            twins[k].wait_recv()
            ready.append(at)
        dense(ready)
        ready = []
    sent += along + across + twins

    sum_by_slot(table, 4, acc_wide, lambda s: jnp.dot(second[table[3, s]], values[s], preferred_element_type=F32))
    mine, theirs = me.xl * 8, (1 - me.xl) * 8

    def scores(at):
        return acc_wide[table[5, at]]

    hops = []
    for i, step in enumerate(OFFSETS + (0,)):
        at = me.along_y(step)
        to_x[at] = scores(theirs + at).astype(BF16)
        hops.append(send(to_x.at[at], from_x.at[at], x_send.at[i], x_recv.at[i], me.lo_peer()))
    rounds = []
    for i, step in enumerate(OFFSETS):
        at = me.along_y(step)
        hops[i].wait_recv()
        to_y[at] = (scores(mine + at) + from_x[at].astype(F32)).astype(BF16)
        rounds.append(send(to_y.at[at], from_y.at[i], y_send.at[i], y_recv.at[i], me.y_peer(step)))
    hops[7].wait_recv()
    total = scores(mine + me.y) + from_x[me.y].astype(F32)
    for i in range(7):
        rounds[i].wait_recv()
        total = total + from_y[i].astype(F32)
    sent += hops + rounds
    kind = lax.broadcasted_iota(jnp.int32, (WIDE, BLOCK), 0)
    live = kind < CLASSES
    shown = jnp.where(live, total, -jnp.inf)
    top = jnp.max(shown, axis=0, keepdims=True)
    expo = jnp.where(live, jnp.exp(shown - top), 0.0)
    norm = jnp.sum(expo, axis=0, keepdims=True)
    grads[...] = (expo / norm - (kind == labels[...]).astype(F32)).astype(BF16)

    def write_logits():
        logits_t[...] = total[:CLASSES]

    sent += gather_row(me, grads, panel_wide, ay_send, ay_recv, ax_send, ax_recv, write_logits)

    sum_by_slot(table, 1, acc_wide, lambda s: lax.dot_general(
        panel_wide[table[0, s]], values[s], (((1,), (1,)), ((), ())), preferred_element_type=F32))
    acc_first[...] = jnp.zeros_like(acc_first)
    acc_second[...] = jnp.zeros_like(acc_second)

    def backward(i, carry):
        for k in range(4):
            grad[:, k * BLOCK:(k + 1) * BLOCK] = acc_wide[table[2, i * 4 + k]].astype(BF16)
        at = pl.ds(i * 4, 4)
        kept = hidden[at].reshape(512, 512)
        back_in = grad[...]
        back = lax.dot_general(back_in, w2[...], (((0,), (0,)), ((), ())), preferred_element_type=F32)
        pre = jnp.where(kept.astype(F32) > 0.0, back, 0.0).astype(BF16)
        acc_first[...] += lax.dot_general(agg[at].reshape(512, 128), pre, (((0,), (0,)), ((), ())), preferred_element_type=F32)
        acc_second[...] += jnp.dot(back_in, kept, preferred_element_type=F32)
        return carry

    lax.fori_loop(0, 8, backward, 0)
    for q in range(4):
        b_in[q * BLOCK:(q + 1) * BLOCK, :] = acc_first[:, q * BLOCK:(q + 1) * BLOCK]
        a_in[q * 192:q * 192 + WIDE, :] = acc_second[:, q * BLOCK:(q + 1) * BLOCK]
        a_in[q * 192 + WIDE:(q + 1) * 192, :] = jnp.zeros((16, BLOCK), F32)
    reduce_all(me, a_in, b_in, a_out, b_out, a_twin, b_twin, a_half, b_half, a_cut, b_cut, a_got, b_got, a_all, b_all,
               send_sem, recv_sem)
    for copy in sent:
        copy.wait_send()


def finish(logits_in, b_out, a_out, logits_t, first_out, second_out):
    logits_t[...] = logits_in[...]
    for q in range(4):
        first_out[:, q * BLOCK:(q + 1) * BLOCK] = b_out[q * BLOCK:(q + 1) * BLOCK, :]
        second_out[:, q * BLOCK:(q + 1) * BLOCK] = a_out[q * 192:q * 192 + CLASSES, :]


def vm(*dims, dtype=BF16):
    return pltpu.VMEM(dims, dtype)


def shards(features, block_ids, block_values, block_count, labels, w_first, w_second):
    scratch = [
        vm(8, 128, dtype=jnp.int32), vm(8, 128, dtype=jnp.int32), pltpu.SMEM((8, 128), jnp.int32),
        vm(32, 128, 128), vm(128, 512), vm(WIDE, 512), vm(16, 128, 128), vm(33, 128, 128, dtype=F32),
        vm(16, 128, 128, dtype=F32), vm(16, 128, 128, dtype=F32), vm(8, 144, 128), vm(8, 144, 128), vm(8, 144, 128),
        vm(7, 144, 128), vm(32, 128, 128), vm(32, 128, 512), vm(32, WIDE, 128), vm(33, WIDE, 128, dtype=F32),
        vm(8, WIDE, 128), vm(8, WIDE, 128), vm(8, WIDE, 128), vm(7, WIDE, 128), vm(WIDE, 128),
        vm(16, WIDE, 128), vm(WIDE, 512), vm(128, 512, dtype=F32), vm(WIDE, 512, dtype=F32),
        vm(768, 128, dtype=F32), vm(512, 128, dtype=F32),
        vm(384, 128, dtype=F32), vm(256, 128, dtype=F32), vm(384, 128, dtype=F32), vm(256, 128, dtype=F32),
        vm(16, 24, 128), vm(16, 16, 128), vm(15, 24, 128), vm(15, 16, 128), vm(16, 24, 128), vm(16, 16, 128),
        DMA((4,)), DMA((8,)), DMA((7,)), DMA((8,)), DMA((8,)), DMA((2,)), DMA((2,)), DMA((8,)), DMA((8,)), DMA((7,)), DMA((7,)),
        DMA((16,)), DMA((16,)), DMA((8,)), DMA((8,)), DMA((7,)), DMA((7,)), DMA((8,)), DMA((8,)), DMA((7,)), DMA((7,)),
        DMA((8,)), DMA((8,)), DMA((8,)), DMA((7,)), DMA((5, 2)), DMA((5, 2)),
    ]
    parts = pl.pallas_call(
        everything,
        out_shape=(jax.ShapeDtypeStruct((CLASSES, 128), F32), jax.ShapeDtypeStruct((512, 128), F32),
                   jax.ShapeDtypeStruct((768, 128), F32)),
        in_specs=[ANY, SM, VM, SM, ANY, VM, ANY, VM],
        out_specs=(VM, VM, VM),
        scratch_shapes=scratch,
        compiler_params=pltpu.CompilerParams(vmem_limit_bytes=60 * 1024 * 1024, collective_id=0, has_side_effects=True),
        name="everything",
    )(features, block_ids[0], block_ids[0], block_count, block_values, labels[None], w_first, w_second.T)
    logits_t, grad_first, second_t = pl.pallas_call(
        finish,
        out_shape=(jax.ShapeDtypeStruct((CLASSES, 128), F32), jax.ShapeDtypeStruct((128, 512), F32),
                   jax.ShapeDtypeStruct((CLASSES, 512), F32)),
        in_specs=[VM, VM, VM],
        out_specs=(VM, VM, VM),
        name="finish",
    )(*parts)
    return logits_t.T, grad_first, second_t.T


def solution(mesh):
    in_specs = (
        P(("col", "row"), None),
        P("row", "col", None),
        P("row", "col", None, None, None),
        P("row", "col"),
        P(("col", "row")),
        P(),
        P(),
    )
    out_specs = (P(("col", "row"), None), P(), P())
    return jax.shard_map(shards, mesh=mesh, in_specs=in_specs, out_specs=out_specs, check_vma=False)
```

time: 827 us -> 125 us (0.15)
  waiting for transfers between devices: 699 us -> 0 us
  Pallas kernels: 0 us -> 123 us
  blocking collectives: 59.1 us -> 0 us
  local copies, waits for them, and re-layouts: 20.6 us -> 0 us
  other arithmetic: 18.9 us -> 0 us
  matrix products: 13.5 us -> 0 us
  between operations: 14.7 us -> 1.29 us
    psum x1 -> x0, waiting for transfers between devices: 279 us -> none  [shards(): lax.psum((part_first, part_second), ('row', 'col'))]
    reduce_scatter x2 -> x0, waiting for transfers between devices: 193 us -> none  [the longest x1 132 us: shards(): lax.psum_scatter(first_term, 'col', scatter_dimension=0, tiled=True)]
    unnamed x6 -> x0, waiting for transfers between devices: 142 us -> none
    pallas_call x0 -> x2, Pallas kernels: none -> 123 us  [the longest x1 121 us: shards(): pl.pallas_call(everything, out_shape=(jax.ShapeDtypeStruct((CLASSES, 128)...]
    all_gather x1 -> x0, waiting for transfers between devices: 84.2 us -> none  [shards(): row_second = lax.all_gather(second_in, 'col', axis=0, tiled=True)]
    all_gather x2 -> x0, blocking collectives: 59.1 us -> none  [the longest x1 31 us: shards(): col_features = lax.all_gather(features, 'row', axis=0, tiled=True)]
    scatter-add x3 -> x0, other arithmetic: 15.4 us -> none  [the longest x2 10 us: forward_term(): jax.ops.segment_sum(products, block_ids // col_blocks, num_segments=row_b...]
    dot_general x7 -> x0, matrix products: 13.5 us -> none  [the longest x2 4.4 us: forward_term(): jnp.einsum('bij,bjf->bif', values, picked, preferred_element_type=jnp.flo...]
  transfers between devices with their start and end apart: 5 -> 0, of which waited for: 5 -> 0; matrix products, arithmetic and copies ran while one was open for 0% -> 0% of each run, Pallas kernels for 0% -> 0%
where the time goes in v1:
time: 125 us
  Pallas kernels  123 us (98%)
  between operations  1.29 us (1%)
    pallas_call x1, Pallas kernels, shards(): pl.pallas_call(everything, out_shape=(jax.ShapeDtypeStruct((CLASSES, 128)...  121 us

profile of v1, /device:TPU:1, one launch (start us, length us, event | category | flops | bytes accessed | tf_op | source)
XLA Modules:
  0.0 124.7 jit_solution(14433332334414477201)
XLA Ops:
  1.3 121.4 %everything.1 = (f32[172,128]{1,0:T(8,128)}, f32[512,128]{1,0:T(8,128)}, f32[768,128]{1,0:T(8,128)}) custom-call(bf16[128,128]{1,0:T(8,128)(2,1)} %features.1, s32[1,32]{1,0:T(1,128)} %bitcast.6, s32[1,32]{1,0:T(1,128)} %bitcast.7, s32[1,1]{1,0:T(1,128)S(6)} %copy.10.count, bf16[1,1,32,128,128]{4,3,2,1,0:T(8,128)(2,1)} %values_any.1, s32[1,128]{1,0:T(1,128)} %bitcast.8, ...), custom_call_target="tpu_custom_call" | custom-call | tf_op jit(solution)/shard_map/everything/pallas_call | solution.py:407
  122.7 2.0 %finish.1 = (f32[172,128]{1,0:T(8,128)}, f32[128,512]{1,0:T(8,128)}, f32[172,512]{1,0:T(8,128)}) custom-call(f32[172,128]{1,0:T(8,128)} %get-tuple-element.9.logits_in, f32[512,128]{1,0:T(8,128)} %get-tuple-element.10.b_out, f32[768,128]{1,0:T(8,128)} %get-tuple-element.11.a_out), custom_call_target="tpu_custom_call" | custom-call | tf_op jit(solution)/shard_map/finish/pallas_call | solution.py:417
